TPU v7x, 512 devices: a whole 4x4x16 slice. The times are simulated.
512 devices in a mesh: seq: 128 (over z, x, core), dp: 4 (over y).
Axes of the slice: x: 4, y: 4, z: 16, core: 2. Of those that a mesh axis runs over, the one named last changes fastest.
Arguments:
- queries: bfloat16 [8192, 512], P(('dp', 'seq')), parts along dimension 0, may hold values from -6 to 6
- keys: bfloat16 [8192, 512], P(('dp', 'seq')), parts along dimension 0, may hold values from -6 to 6
- values: bfloat16 [8192, 512], P(('dp', 'seq')), parts along dimension 0, may hold values from -6 to 6
- residual: bfloat16 [8192, 1024], P(('dp', 'seq')), parts along dimension 0, may hold values from -16 to 16
- lengths: int32 [4], P('dp'), parts along dimension 0, may hold values from 1024 to 2048
- out_proj: bfloat16 [512, 1024], replicated, may hold values from -0.75 to 0.75
- ln_gain: float32 [1024], replicated, may hold values from 0.1 to 1.9
- ln_bias: float32 [1024], replicated, may hold values from -3 to 3
- conv_in: bfloat16 [1024, 1024], replicated, may hold values from -0.1875 to 0.1875
- taps: float32 [31, 512], replicated, may hold values from -1 to 1
- bn_scale: float32 [512], replicated, may hold values from 0.5 to 2
- bn_shift: float32 [512], replicated, may hold values from -3 to 3
- conv_out: bfloat16 [512, 1024], replicated, may hold values from -0.25 to 0.25
Outputs:
- block_out: bfloat16 [8192, 1024], P(('dp', 'seq')), parts along dimension 0
There are 4 independent parts, one for each index of `dp`. A program takes and returns all parts, laid end to end along the dimension named above; an argument that names none is the same for every part. Nothing has to cross between parts.
All inputs are finite; a program needn't handle non-finite values.
Results may differ from a plain program's by a relative error of at most 0.0075.
Values may be sent and summed in bfloat16 or wider, within the bound.
A program may use at most 64 MiB of HBM per device.

v0:
```python
import math
import jax
import jax.numpy as jnp
from jax import lax
from jax.sharding import PartitionSpec as P

HEAD_DIM = 64


def extended(block, sides, width):
    for axis, dim in sides:
        count = lax.axis_size(axis)
        forward = [(i, i + 1) for i in range(count - 1)]
        backward = [(target, source) for source, target in forward]
        low = lax.ppermute(
            lax.slice_in_dim(block, block.shape[dim] - width, None, axis=dim), axis, forward
        )
        high = lax.ppermute(lax.slice_in_dim(block, 0, width, axis=dim), axis, backward)
        block = jnp.concatenate([low, block, high], axis=dim)
    return block


def norm_lift(rows, row_frames, limit, ln_gain, ln_bias, conv_in):
    average = jnp.mean(rows, axis=-1, keepdims=True)
    centred = rows - average
    variance = jnp.mean(centred * centred, axis=-1, keepdims=True)
    normed = (centred * lax.rsqrt(variance + 1e-05) * ln_gain + ln_bias).astype(jnp.bfloat16)
    lifted = jnp.dot(normed, conv_in, preferred_element_type=jnp.float32)
    channels = conv_in.shape[1] // 2
    inside = ((row_frames >= 0) & (row_frames < limit)).astype(jnp.float32)
    return (inside[:, None] * lifted[:, :channels] * jax.nn.sigmoid(lifted[:, channels:])).astype(
        jnp.bfloat16
    )


def attend(carried, query_rows, key_block, value_block, key_frames, limit):
    running, totals, weighted = carried
    factor = 1.0 / math.sqrt(query_rows.shape[2])
    scores = (
        jnp.einsum("qhd,khd->hqk", query_rows, key_block, preferred_element_type=jnp.float32)
        * factor
    )
    scores = jnp.where((key_frames < limit)[None, None, :], scores, -1e30)
    highest = jnp.maximum(running, jnp.max(scores, axis=-1))
    rescale = jnp.exp(running - highest)
    powered = jnp.exp(scores - highest[:, :, None])
    totals = totals * rescale + jnp.sum(powered, axis=-1)
    weighted = weighted * jnp.transpose(rescale)[:, :, None] + jnp.einsum(
        "hqk,khd->qhd",
        powered.astype(jnp.bfloat16),
        value_block,
        preferred_element_type=jnp.float32,
    )
    return (highest, totals, weighted)


def split_pair(packed, columns, heads_here):
    row_count = packed.shape[0]
    key_part = packed[:, 0, :columns].reshape(row_count, heads_here, columns // heads_here)
    value_part = packed[:, 0, columns:].reshape(row_count, heads_here, columns // heads_here)
    return (key_part, value_part)


def on_device(
    queries,
    keys,
    values,
    residual,
    lengths,
    out_proj,
    ln_gain,
    ln_bias,
    conv_in,
    taps,
    bn_scale,
    bn_shift,
    conv_out,
):
    frames_here = residual.shape[0]
    width_att = queries.shape[1]
    devices = lax.axis_size("seq")
    position = lax.axis_index("seq")
    heads_all = width_att // HEAD_DIM
    groups = min(devices, heads_all)
    copies = devices // groups
    heads_here = heads_all // groups
    columns = heads_here * HEAD_DIM
    sub_rows = frames_here // copies
    query_count = devices * sub_rows
    limit = lengths[0]
    local_frames = position * frames_here + jnp.arange(frames_here, dtype=jnp.int32)
    valid_local = (local_frames < limit).astype(jnp.float32)
    query_rows = lax.all_to_all(
        queries.reshape(sub_rows, devices, columns), "seq", split_axis=1, concat_axis=0, tiled=True
    )
    carried = (
        jnp.full((heads_here, query_count), -1e30, jnp.float32),
        jnp.zeros((heads_here, query_count), jnp.float32),
        jnp.zeros((query_count, heads_here, HEAD_DIM), jnp.float32),
    )
    paired = jnp.concatenate(
        [
            keys.reshape(frames_here, 1, groups, columns),
            values.reshape(frames_here, 1, groups, columns),
        ],
        axis=3,
    )
    paired = jnp.broadcast_to(paired, (frames_here, copies, groups, 2 * columns)).reshape(
        frames_here, devices, 2 * columns
    )
    all_pairs = lax.all_to_all(paired, "seq", split_axis=1, concat_axis=0, tiled=True)
    block_size = groups * frames_here
    block_count = (limit + block_size - 1) // block_size

    def visit(number, looped):
        start = number * block_size
        current = lax.dynamic_slice_in_dim(all_pairs, start, block_size, 0)
        key_block, value_block = split_pair(current, columns, heads_here)
        key_frames = start + jnp.arange(block_size, dtype=jnp.int32)
        return attend(looped, query_rows, key_block, value_block, key_frames, limit)

    carried = lax.fori_loop(0, block_count, visit, carried)
    running, totals, weighted = carried
    context = (weighted / jnp.transpose(totals)[:, :, None]).astype(jnp.bfloat16)
    returned = lax.all_to_all(
        context.reshape(devices, sub_rows, 1, columns),
        "seq",
        split_axis=0,
        concat_axis=2,
        tiled=True,
    )
    context_here = returned.reshape(frames_here, width_att)
    mixed = residual.astype(jnp.float32) + valid_local[:, None] * jnp.dot(
        context_here, out_proj, preferred_element_type=jnp.float32
    )
    margin = taps.shape[0] // 2
    gated = norm_lift(mixed, local_frames, limit, ln_gain, ln_bias, conv_in)
    widened = extended(gated, (("seq", 0),), margin)
    widened = widened.astype(jnp.float32)
    filtered = taps[0] * widened[0:frames_here]
    for offset in range(1, taps.shape[0]):
        filtered = filtered + taps[offset] * widened[offset : offset + frames_here]
    shifted = filtered * bn_scale + bn_shift
    activated = (shifted * jax.nn.sigmoid(shifted)).astype(jnp.bfloat16)
    return (mixed + jnp.dot(activated, conv_out, preferred_element_type=jnp.float32)).astype(
        jnp.bfloat16
    )


def solution(mesh):
    placed = (
        P(("dp", "seq"), None),
        P(("dp", "seq"), None),
        P(("dp", "seq"), None),
        P(("dp", "seq"), None),
        P("dp"),
        P(),
        P(),
        P(),
        P(),
        P(),
        P(),
        P(),
        P(),
    )
    return jax.shard_map(
        on_device, mesh=mesh, in_specs=placed, out_specs=P(("dp", "seq"), None), check_vma=False
    )
```

profile of v0, /device:TPU:31, one launch (start us, length us, event | category | flops | bytes accessed | tf_op | source)
XLA Modules:
  0.0 132.5 jit_solution(11860965346838346635)
XLA Ops:
  0.0 1.6 %reshape.94 = bf16[1,128,64]{2,0,1:T(2,128)(2,1)} reshape(bf16[16,512]{1,0:T(8,128)(2,1)} %param.15) | data formatting | bytes 32768 | tf_op jit(solution)/shard_map/reshape | solution.py:94
  1.6 19.7 %all-to-all-start.1 = ((bf16[1,128,64]{2,0,1:T(2,128)(2,1)}), bf16[1,128,64]{2,0,1:T(2,128)(2,1)S(1)}, u32[]{:S(2)}, u32[]{:S(2)}) async-start(bf16[1,128,64]{2,0,1:T(2,128)(2,1)} %reshape.94), calls=%async_computation.1 | async-start | bytes 131072 | tf_op jit(solution)/shard_map/all_to_all | solution.py:93
  21.3 0.8 reshape.88
  22.1 0.8 reshape.89
  23.0 11.7 %all-to-all-done.1 = bf16[1,128,64]{2,0,1:T(2,128)(2,1)S(1)} async-done(((bf16[1,128,64]{2,0,1:T(2,128)(2,1)}), bf16[1,128,64]{2,0,1:T(2,128)(2,1)S(1)}, u32[]{:S(2)}, u32[]{:S(2)}) %all-to-all-start.1) | async-done | bytes 16416 | tf_op jit(solution)/shard_map/all_to_all | solution.py:93
  34.7 0.9 broadcast_in_dim.42
  35.6 7.2 %all-to-all-start = ((bf16[16,128,128]{2,0,1:T(8,128)(2,1)}), bf16[16,128,128]{2,0,1:T(8,128)(2,1)S(1)}, u32[]{:S(2)}, u32[]{:S(2)}) async-start(bf16[16,128,128]{2,0,1:T(8,128)(2,1)} %bitcast.11), calls=%async_computation | async-start | bytes 1048576 | tf_op jit(solution)/shard_map/all_to_all | solution.py:111
  43.7 32.1 %all-to-all-done = bf16[16,128,128]{2,0,1:T(8,128)(2,1)S(1)} async-done(((bf16[16,128,128]{2,0,1:T(8,128)(2,1)}), bf16[16,128,128]{2,0,1:T(8,128)(2,1)S(1)}, u32[]{:S(2)}, u32[]{:S(2)}) %all-to-all-start) | async-done | bytes 524320 | tf_op jit(solution)/shard_map/all_to_all | solution.py:111
  75.8 18.8 %while.14 = (s32[]{:T(128)}, f32[1,128]{1,0:T(1,128)S(1)}, f32[1,128]{1,0:T(1,128)S(1)}, f32[128,1,64]{0,2,1:T(8,128)S(1)}, s32[]{:T(128)}, /*index=5*/s32[]{:T(...) while((s32[]{:T(128)}, f32[1,128]{1,0:T(1,128)S(1)}, ...), condition=%wide.region_3.4_spmd, body=%wide.region_0.3_spmd.sunk | while | flops 4326023 | bytes 353099 | solution.py:122
  75.8 0.7 add_compare_fusion.2
  76.6 0.3 fusion.108
  77.0 0.7 add_compare_fusion.2
  77.8 0.3 fusion.108
  78.1 0.7 add_compare_fusion.2
  79.0 0.3 fusion.108
  79.3 0.7 add_compare_fusion.2
  80.1 0.3 fusion.108
  80.5 0.7 add_compare_fusion.2
  81.3 0.3 fusion.108
  81.7 0.7 add_compare_fusion.2
  82.5 0.3 fusion.108
  82.9 0.7 add_compare_fusion.2
  83.7 0.3 fusion.108
  84.0 0.7 add_compare_fusion.2
  84.9 0.3 fusion.108
  85.2 0.7 add_compare_fusion.2
  86.0 0.3 fusion.108
  86.4 0.7 add_compare_fusion.2
  87.2 0.3 fusion.108
  87.6 0.7 add_compare_fusion.2
  88.4 0.3 fusion.108
  88.7 0.7 add_compare_fusion.2
  89.6 0.3 fusion.108
  89.9 0.7 add_compare_fusion.2
  90.7 0.3 fusion.108
  91.1 0.7 add_compare_fusion.2
  92.3 0.7 add_compare_fusion.2
  93.4 0.7 add_compare_fusion.2
  94.3 0.3 fusion.108
  94.6 0.7 copy.28
  95.4 7.2 %all-to-all-start.2 = ((bf16[128,1,1,64]{3,2,1,0:T(2,128)(2,1)}), bf16[128,1,1,64]{3,2,1,0:T(2,128)(2,1)S(1)}, u32[]{:S(2)}, u32[]{:S(2)}) async-start(bf16[128,1,1,64]{3,2,1,0:T(2,128)(2,1)} %copy.28), calls=%async_computation.2 | async-start | bytes 131072 | tf_op jit(solution)/shard_map/all_to_all | solution.py:125
  102.6 13.4 %all-to-all-done.2 = bf16[128,1,1,64]{3,2,1,0:T(2,128)(2,1)S(1)} async-done(((bf16[128,1,1,64]{3,2,1,0:T(2,128)(2,1)}), bf16[128,1,1,64]{3,2,1,0:T(2,128)(2,1)S(1)}, u32[]{:S(2)}, u32[]{:S(2)}) %all-to-all-start.2) | async-done | bytes 16416 | tf_op jit(solution)/shard_map/all_to_all | solution.py:125
  116.3 1.6 %fusion.94 = (f32[16]{0:T(128)S(1)}, f32[16,1024]{1,0:T(8,128)S(1)}) fusion(bf16[16,512]{1,0:T(8,128)(2,1)S(1)} %reshape.93, bf16[512,1024]{1,0:T(8,128)(2,1)} %param.20, f32[16]{0:T(128)S(1)} %compare_convert_fusion, bf16[16,1024]{1,0:T(8,128)(2,1)S(1)} %copy-done.2), kind=kOutput, calls=%fused_computation.148 | convolution fusion | flops 16842736 | bytes 1163392 | tf_op jit(solution)/shard_map/dot_general | solution.py:133
  118.1 0.4 fusion.12
  118.7 4.3 %collective-permute-start = (bf16[15,512]{1,0:T(8,128)(2,1)S(1)}, bf16[15,512]{1,0:T(8,128)(2,1)S(1)}, u32[]{:S(2)}, u32[]{:S(2)}) collective-permute-start(bf16[15,512]{1,0:T(8,128)(2,1)S(1)} %get-tuple-element.126), channel_id=1, source_target_pairs={{0,4},{4,8},{8,12},{12,16},{16,20},{20,24},{24,28},{28,32},{32,36}... | collective-permute-start | bytes 46088 | tf_op jit(solution)/shard_map/ppermute | solution.py:15
  123.0 1.9 %collective-permute-start.1 = (bf16[15,512]{1,0:T(8,128)(2,1)S(1)}, bf16[15,512]{1,0:T(8,128)(2,1)S(1)}, u32[]{:S(2)}, u32[]{:S(2)}) collective-permute-start(bf16[15,512]{1,0:T(8,128)(2,1)S(1)} %get-tuple-element.127), channel_id=1, source_target_pairs={{4,0},{8,4},{12,8},{16,12},{20,16},{24,20},{28,24},{32,28},{36,32}... | collective-permute-start | bytes 46088 | tf_op jit(solution)/shard_map/ppermute | solution.py:18
  125.0 5.2 %collective-permute-done.1 = bf16[15,512]{1,0:T(8,128)(2,1)S(1)} collective-permute-done((bf16[15,512]{1,0:T(8,128)(2,1)S(1)}, bf16[15,512]{1,0:T(8,128)(2,1)S(1)}, u32[]{:S(2)}, u32[]{:S(2)}) %collective-permute-start.1) | collective-permute-done | bytes 15392 | tf_op jit(solution)/shard_map/ppermute | solution.py:18
  130.2 2.3 %fusion.11 = bf16[16,1024]{1,0:T(8,128)(2,1)} fusion(f32[16,1024]{1,0:T(8,128)S(1)} %get-tuple-element.129, bf16[512,1024]{1,0:T(8,128)(2,1)} %param.27, f32[46,512]{1,0:T(8,128)S(1)} %maximum_convert_fusion, f32[512]{0:T(512)S(1)} %copy-done.5, f32[512]{0:T(512)S(1)} %copy-done.6, f32[512]{0:T(512)S(1)} %bitcast.128, f32[512]{0:T(512)S(1)} %bitcast.129, ...), kind=kOutput, calls=%fused_computation.21 | convolution fusion | flops 17367040 | bytes 2230272 | tf_op jit(solution)/shard_map/dot_general | solution.py:145
  (116 shorter events, 5.0 us)
Async XLA Ops:
  0.0 118.1 %copy-start = (bf16[1024,1024]{1,0:T(8,128)(2,1)S(1)}, bf16[1024,1024]{1,0:T(8,128)(2,1)}, u32[]{:S(2)}) copy-start(bf16[1024,1024]{1,0:T(8,128)(2,1)} %param.23) | copy-start | bytes 6291460
  0.0 43.5 %copy-start.1 = (f32[31,512]{1,0:T(8,128)S(1)}, f32[31,512]{1,0:T(8,128)}, u32[]{:S(2)}) copy-start(f32[31,512]{1,0:T(8,128)} %param.24) | copy-start | bytes 190468
  1.6 33.1 %all-to-all-start.1 = ((bf16[1,128,64]{2,0,1:T(2,128)(2,1)}), bf16[1,128,64]{2,0,1:T(2,128)(2,1)S(1)}, u32[]{:S(2)}, u32[]{:S(2)}) async-start(bf16[1,128,64]{2,0,1:T(2,128)(2,1)} %reshape.94), calls=%async_computation.1 | async-start | bytes 131072 | tf_op jit(solution)/shard_map/all_to_all | solution.py:93
  23.0 93.3 %copy-start.2 = (bf16[16,1024]{1,0:T(8,128)(2,1)S(1)}, bf16[16,1024]{1,0:T(8,128)(2,1)}, u32[]{:S(2)}) copy-start(bf16[16,1024]{1,0:T(8,128)(2,1)} %param.18) | copy-start | bytes 98308
  35.6 40.2 %all-to-all-start = ((bf16[16,128,128]{2,0,1:T(8,128)(2,1)}), bf16[16,128,128]{2,0,1:T(8,128)(2,1)S(1)}, u32[]{:S(2)}, u32[]{:S(2)}) async-start(bf16[16,128,128]{2,0,1:T(8,128)(2,1)} %bitcast.11), calls=%async_computation | async-start | bytes 1048576 | tf_op jit(solution)/shard_map/all_to_all | solution.py:111
  42.8 75.3 %copy-start.3 = (f32[1024]{0:T(1024)S(1)}, f32[1024]{0:T(1024)}, u32[]{:S(2)}) copy-start(f32[1024]{0:T(1024)} %param.22) | copy-start | bytes 12292
  42.8 75.3 %copy-start.4 = (f32[1024]{0:T(1024)S(1)}, f32[1024]{0:T(1024)}, u32[]{:S(2)}) copy-start(f32[1024]{0:T(1024)} %param.21) | copy-start | bytes 12292
  95.4 34.8 %copy-start.5 = (f32[512]{0:T(512)S(1)}, f32[512]{0:T(512)}, u32[]{:S(2)}) copy-start(f32[512]{0:T(512)} %param.26) | copy-start | bytes 6148
  95.4 34.8 %copy-start.6 = (f32[512]{0:T(512)S(1)}, f32[512]{0:T(512)}, u32[]{:S(2)}) copy-start(f32[512]{0:T(512)} %param.25) | copy-start | bytes 6148
  95.4 20.6 %all-to-all-start.2 = ((bf16[128,1,1,64]{3,2,1,0:T(2,128)(2,1)}), bf16[128,1,1,64]{3,2,1,0:T(2,128)(2,1)S(1)}, u32[]{:S(2)}, u32[]{:S(2)}) async-start(bf16[128,1,1,64]{3,2,1,0:T(2,128)(2,1)} %copy.28), calls=%async_computation.2 | async-start | bytes 131072 | tf_op jit(solution)/shard_map/all_to_all | solution.py:125
  118.7 6.3 %collective-permute-start = (bf16[15,512]{1,0:T(8,128)(2,1)S(1)}, bf16[15,512]{1,0:T(8,128)(2,1)S(1)}, u32[]{:S(2)}, u32[]{:S(2)}) collective-permute-start(bf16[15,512]{1,0:T(8,128)(2,1)S(1)} %get-tuple-element.126), channel_id=1, source_target_pairs={{0,4},{4,8},{8,12},{12,16},{16,20},{20,24},{24,28},{28,32},{32,36}... | collective-permute-start | bytes 46088 | tf_op jit(solution)/shard_map/ppermute | solution.py:15
  123.0 7.2 %collective-permute-start.1 = (bf16[15,512]{1,0:T(8,128)(2,1)S(1)}, bf16[15,512]{1,0:T(8,128)(2,1)S(1)}, u32[]{:S(2)}, u32[]{:S(2)}) collective-permute-start(bf16[15,512]{1,0:T(8,128)(2,1)S(1)} %get-tuple-element.127), channel_id=1, source_target_pairs={{4,0},{8,4},{12,8},{16,12},{20,16},{24,20},{28,24},{32,28},{36,32}... | collective-permute-start | bytes 46088 | tf_op jit(solution)/shard_map/ppermute | solution.py:18
where the time goes:
time: 133 us; the launch traced here: 132 us
  waiting for transfers between devices  62.4 us (47%)
  starting transfers between devices  40.3 us (30%)
  other arithmetic  12.2 us (9%)
  matrix products  10.9 us (8%)
  local copies, waits for them, and re-layouts  5.18 us (4%)
    all_to_all x1, waiting for transfers between devices, on_device(): lax.all_to_all(paired, 'seq', split_axis=1, concat_axis=0, tiled=True)  32.1 us
    all_to_all x1, starting transfers between devices, on_device(): lax.all_to_all(queries.reshape(sub_rows, devices, columns), 'seq', split_...  19.7 us
    all_to_all x1, waiting for transfers between devices, on_device(): lax.all_to_all(context.reshape(devices, sub_rows, 1, columns), 'seq', spl...  13.4 us
    all_to_all x1, waiting for transfers between devices, on_device(): lax.all_to_all(queries.reshape(sub_rows, devices, columns), 'seq', split_...  11.7 us
    lt x16, other arithmetic, attend(): scores = jnp.where((key_frames < limit)[None, None, :], scores, -1e+30)  10.5 us
    all_to_all x1, starting transfers between devices, on_device(): lax.all_to_all(context.reshape(devices, sub_rows, 1, columns), 'seq', spl...  7.21 us
    all_to_all x1, starting transfers between devices, on_device(): lax.all_to_all(paired, 'seq', split_axis=1, concat_axis=0, tiled=True)  7.2 us
    ppermute x1, waiting for transfers between devices, extended(): lax.ppermute(lax.slice_in_dim(block, 0, width, axis=dim), axis, backward)  5.2 us
  transfers between devices with their start and end apart: 5, of which 4 were waited for; matrix products, arithmetic and copies ran while one was open for 1% of the time, Pallas kernels for 0%

commit v1 on v0

--- a/solution.py
+++ b/solution.py
@@ -90,9 +90,12 @@
     limit = lengths[0]
     local_frames = position * frames_here + jnp.arange(frames_here, dtype=jnp.int32)
     valid_local = (local_frames < limit).astype(jnp.float32)
-    query_rows = lax.all_to_all(
-        queries.reshape(sub_rows, devices, columns), "seq", split_axis=1, concat_axis=0, tiled=True
-    )
+    slab_in = queries.reshape(sub_rows, devices, columns)
+    before = jax.lax.axis_size("seq")
+    after = jnp.split(slab_in, before, axis=1)
+    upper = jnp.stack(after)
+    now = jax.lax.all_to_all(upper, "seq", 0, 0)
+    query_rows = jnp.concatenate(now, axis=0)
     carried = (
         jnp.full((heads_here, query_count), -1e30, jnp.float32),
         jnp.zeros((heads_here, query_count), jnp.float32),

time: 133 us -> 203 us (1.53)
  local copies, waits for them, and re-layouts: 5.18 us -> 74.7 us
    unnamed x14 -> x141, local copies, waits for them, and re-layouts: 0.03 us -> 69.6 us
where the time goes in v1:
time: 203 us; the launch traced here: 202 us
  local copies, waits for them, and re-layouts  74.7 us (37%)
  waiting for transfers between devices  62.4 us (31%)
  starting transfers between devices  40.3 us (20%)
  other arithmetic  12.2 us (6%)
  matrix products  10.9 us (5%)
    unnamed x141, local copies, waits for them, and re-layouts  69.6 us
    all_to_all x1, waiting for transfers between devices, on_device(): lax.all_to_all(paired, 'seq', split_axis=1, concat_axis=0, tiled=True)  32.1 us
    all_to_all x1, starting transfers between devices, on_device(): now = jax.lax.all_to_all(upper, 'seq', 0, 0)  19.7 us
    all_to_all x1, waiting for transfers between devices, on_device(): lax.all_to_all(context.reshape(devices, sub_rows, 1, columns), 'seq', spl...  13.4 us
    all_to_all x1, waiting for transfers between devices, on_device(): now = jax.lax.all_to_all(upper, 'seq', 0, 0)  11.7 us
    lt x16, other arithmetic, attend(): scores = jnp.where((key_frames < limit)[None, None, :], scores, -1e+30)  10.5 us
    all_to_all x1, starting transfers between devices, on_device(): lax.all_to_all(context.reshape(devices, sub_rows, 1, columns), 'seq', spl...  7.21 us
    all_to_all x1, starting transfers between devices, on_device(): lax.all_to_all(paired, 'seq', split_axis=1, concat_axis=0, tiled=True)  7.2 us
  transfers between devices with their start and end apart: 5, of which 4 were waited for; matrix products, arithmetic and copies ran while one was open for 1% of the time, Pallas kernels for 0%

profile of v1, /device:TPU:31, one launch (start us, length us, event | category | flops | bytes accessed | tf_op | source)
XLA Modules:
  0.0 202.0 jit_solution(96357215283600693)
XLA Ops:
  0.0 1.0 reshape.91
  6.9 0.6 constant_dynamic-update-slice_fusion.116
  8.6 0.6 constant_dynamic-update-slice_fusion.113
  13.0 0.6 constant_dynamic-update-slice_fusion.105
  16.3 0.6 constant_dynamic-update-slice_fusion.99
  17.8 0.6 constant_dynamic-update-slice_fusion.96
  20.1 0.6 constant_dynamic-update-slice_fusion.92
  23.4 0.6 constant_dynamic-update-slice_fusion.86
  31.1 0.6 constant_dynamic-update-slice_fusion.72
  44.1 0.6 constant_dynamic-update-slice_fusion.48
  50.7 0.6 constant_dynamic-update-slice_fusion.36
  55.7 0.6 constant_dynamic-update-slice_fusion.27
  57.3 0.6 constant_dynamic-update-slice_fusion.24
  61.2 0.6 constant_dynamic-update-slice_fusion.17
  62.3 0.6 constant_dynamic-update-slice_fusion.15
  67.8 0.6 constant_dynamic-update-slice_fusion.5
  71.2 19.7 %all-to-all-start.1 = ((bf16[128,1,1,64]{3,2,1,0:T(2,128)(2,1)}), bf16[128,1,1,64]{3,2,1,0:T(2,128)(2,1)S(1)}, u32[]{:S(2)}, u32[]{:S(2)}) async-start(bf16[128,1,1,64]{3,2,1,0:T(2,128)(2,1)} %constant_dynamic-update-slice_fusion), calls=%async_computation.1 | async-start | bytes 131072 | tf_op jit(solution)/shard_map/all_to_all | solution.py:97
  90.8 0.8 reshape.88
  91.7 0.8 reshape.89
  92.6 11.7 %all-to-all-done.1 = bf16[128,1,1,64]{3,2,1,0:T(2,128)(2,1)S(1)} async-done(((bf16[128,1,1,64]{3,2,1,0:T(2,128)(2,1)}), bf16[128,1,1,64]{3,2,1,0:T(2,128)(2,1)S(1)}, u32[]{:S(2)}, u32[]{:S(2)}) %all-to-all-start.1) | async-done | bytes 16416 | tf_op jit(solution)/shard_map/all_to_all | solution.py:97
  104.3 0.9 broadcast_in_dim.42
  105.2 7.2 %all-to-all-start = ((bf16[16,128,128]{2,0,1:T(8,128)(2,1)}), bf16[16,128,128]{2,0,1:T(8,128)(2,1)S(1)}, u32[]{:S(2)}, u32[]{:S(2)}) async-start(bf16[16,128,128]{2,0,1:T(8,128)(2,1)} %bitcast.11), calls=%async_computation | async-start | bytes 1048576 | tf_op jit(solution)/shard_map/all_to_all | solution.py:114
  113.2 32.1 %all-to-all-done = bf16[16,128,128]{2,0,1:T(8,128)(2,1)S(1)} async-done(((bf16[16,128,128]{2,0,1:T(8,128)(2,1)}), bf16[16,128,128]{2,0,1:T(8,128)(2,1)S(1)}, u32[]{:S(2)}, u32[]{:S(2)}) %all-to-all-start) | async-done | bytes 524320 | tf_op jit(solution)/shard_map/all_to_all | solution.py:114
  145.3 18.8 %while.14 = (s32[]{:T(128)}, f32[1,128]{1,0:T(1,128)S(1)}, f32[1,128]{1,0:T(1,128)S(1)}, f32[128,1,64]{0,2,1:T(8,128)S(1)}, s32[]{:T(128)}, /*index=5*/s32[]{:T(...) while((s32[]{:T(128)}, f32[1,128]{1,0:T(1,128)S(1)}, ...), condition=%wide.region_3.4_spmd, body=%wide.region_0.3_spmd.sunk | while | flops 4326023 | bytes 353099 | solution.py:125
  145.3 0.7 add_compare_fusion.2
  146.5 0.7 add_compare_fusion.2
  147.7 0.7 add_compare_fusion.2
  148.9 0.7 add_compare_fusion.2
  150.1 0.7 add_compare_fusion.2
  151.2 0.7 add_compare_fusion.2
  152.4 0.7 add_compare_fusion.2
  153.6 0.7 add_compare_fusion.2
  154.8 0.7 add_compare_fusion.2
  155.9 0.7 add_compare_fusion.2
  157.1 0.7 add_compare_fusion.2
  158.3 0.7 add_compare_fusion.2
  159.5 0.7 add_compare_fusion.2
  160.6 0.7 add_compare_fusion.2
  161.8 0.7 add_compare_fusion.2
  163.0 0.7 add_compare_fusion.2
  164.2 0.7 copy.418
  164.9 7.2 %all-to-all-start.2 = ((bf16[128,1,1,64]{3,2,1,0:T(2,128)(2,1)}), bf16[128,1,1,64]{3,2,1,0:T(2,128)(2,1)S(1)}, u32[]{:S(2)}, u32[]{:S(2)}) async-start(bf16[128,1,1,64]{3,2,1,0:T(2,128)(2,1)} %copy.418), calls=%async_computation.2 | async-start | bytes 131072 | tf_op jit(solution)/shard_map/all_to_all | solution.py:128
  172.1 13.4 %all-to-all-done.2 = bf16[128,1,1,64]{3,2,1,0:T(2,128)(2,1)S(1)} async-done(((bf16[128,1,1,64]{3,2,1,0:T(2,128)(2,1)}), bf16[128,1,1,64]{3,2,1,0:T(2,128)(2,1)S(1)}, u32[]{:S(2)}, u32[]{:S(2)}) %all-to-all-start.2) | async-done | bytes 16416 | tf_op jit(solution)/shard_map/all_to_all | solution.py:128
  185.8 1.6 fusion.94
  188.2 4.3 %collective-permute-start = (bf16[15,512]{1,0:T(8,128)(2,1)S(1)}, bf16[15,512]{1,0:T(8,128)(2,1)S(1)}, u32[]{:S(2)}, u32[]{:S(2)}) collective-permute-start(bf16[15,512]{1,0:T(8,128)(2,1)S(1)} %get-tuple-element.150), channel_id=1, source_target_pairs={{0,4},{4,8},{8,12},{12,16},{16,20},{20,24},{24,28},{28,32},{32,36}... | collective-permute-start | bytes 46088 | tf_op jit(solution)/shard_map/ppermute | solution.py:15
  192.5 1.9 collective-permute-start.1
  194.5 5.2 %collective-permute-done.1 = bf16[15,512]{1,0:T(8,128)(2,1)S(1)} collective-permute-done((bf16[15,512]{1,0:T(8,128)(2,1)S(1)}, bf16[15,512]{1,0:T(8,128)(2,1)S(1)}, u32[]{:S(2)}, u32[]{:S(2)}) %collective-permute-start.1) | collective-permute-done | bytes 15392 | tf_op jit(solution)/shard_map/ppermute | solution.py:18
  199.7 2.3 %fusion.11 = bf16[16,1024]{1,0:T(8,128)(2,1)} fusion(f32[16,1024]{1,0:T(8,128)S(1)} %get-tuple-element.153, bf16[512,1024]{1,0:T(8,128)(2,1)} %param.27, f32[46,512]{1,0:T(8,128)S(1)} %maximum_convert_fusion, f32[512]{0:T(512)S(1)} %copy-done.5, f32[512]{0:T(512)S(1)} %copy-done.6, f32[512]{0:T(512)S(1)} %bitcast.640, f32[512]{0:T(512)S(1)} %bitcast.641, ...), kind=kOutput, calls=%fused_computation.21 | convolution fusion | flops 17367040 | bytes 2230272 | tf_op jit(solution)/shard_map/dot_general | solution.py:148
  (244 shorter events, 70.2 us)
Async XLA Ops:
  0.0 187.7 %copy-start = (bf16[1024,1024]{1,0:T(8,128)(2,1)S(1)}, bf16[1024,1024]{1,0:T(8,128)(2,1)}, u32[]{:S(2)}) copy-start(bf16[1024,1024]{1,0:T(8,128)(2,1)} %param.23) | copy-start | bytes 6291460
  0.0 113.1 %copy-start.1 = (f32[31,512]{1,0:T(8,128)S(1)}, f32[31,512]{1,0:T(8,128)}, u32[]{:S(2)}) copy-start(f32[31,512]{1,0:T(8,128)} %param.24) | copy-start | bytes 190468
  71.2 33.1 %all-to-all-start.1 = ((bf16[128,1,1,64]{3,2,1,0:T(2,128)(2,1)}), bf16[128,1,1,64]{3,2,1,0:T(2,128)(2,1)S(1)}, u32[]{:S(2)}, u32[]{:S(2)}) async-start(bf16[128,1,1,64]{3,2,1,0:T(2,128)(2,1)} %constant_dynamic-update-slice_fusion), calls=%async_computation.1 | async-start | bytes 131072 | tf_op jit(solution)/shard_map/all_to_all | solution.py:97
  92.6 93.3 %copy-start.2 = (bf16[16,1024]{1,0:T(8,128)(2,1)S(1)}, bf16[16,1024]{1,0:T(8,128)(2,1)}, u32[]{:S(2)}) copy-start(bf16[16,1024]{1,0:T(8,128)(2,1)} %param.18) | copy-start | bytes 98308
  105.2 40.2 %all-to-all-start = ((bf16[16,128,128]{2,0,1:T(8,128)(2,1)}), bf16[16,128,128]{2,0,1:T(8,128)(2,1)S(1)}, u32[]{:S(2)}, u32[]{:S(2)}) async-start(bf16[16,128,128]{2,0,1:T(8,128)(2,1)} %bitcast.11), calls=%async_computation | async-start | bytes 1048576 | tf_op jit(solution)/shard_map/all_to_all | solution.py:114
  112.4 75.3 %copy-start.3 = (f32[1024]{0:T(1024)S(1)}, f32[1024]{0:T(1024)}, u32[]{:S(2)}) copy-start(f32[1024]{0:T(1024)} %param.22) | copy-start | bytes 12292
  112.4 75.3 %copy-start.4 = (f32[1024]{0:T(1024)S(1)}, f32[1024]{0:T(1024)}, u32[]{:S(2)}) copy-start(f32[1024]{0:T(1024)} %param.21) | copy-start | bytes 12292
  164.9 34.8 %copy-start.5 = (f32[512]{0:T(512)S(1)}, f32[512]{0:T(512)}, u32[]{:S(2)}) copy-start(f32[512]{0:T(512)} %param.26) | copy-start | bytes 6148
  164.9 34.8 %copy-start.6 = (f32[512]{0:T(512)S(1)}, f32[512]{0:T(512)}, u32[]{:S(2)}) copy-start(f32[512]{0:T(512)} %param.25) | copy-start | bytes 6148
  164.9 20.6 %all-to-all-start.2 = ((bf16[128,1,1,64]{3,2,1,0:T(2,128)(2,1)}), bf16[128,1,1,64]{3,2,1,0:T(2,128)(2,1)S(1)}, u32[]{:S(2)}, u32[]{:S(2)}) async-start(bf16[128,1,1,64]{3,2,1,0:T(2,128)(2,1)} %copy.418), calls=%async_computation.2 | async-start | bytes 131072 | tf_op jit(solution)/shard_map/all_to_all | solution.py:128
  188.2 6.3 %collective-permute-start = (bf16[15,512]{1,0:T(8,128)(2,1)S(1)}, bf16[15,512]{1,0:T(8,128)(2,1)S(1)}, u32[]{:S(2)}, u32[]{:S(2)}) collective-permute-start(bf16[15,512]{1,0:T(8,128)(2,1)S(1)} %get-tuple-element.150), channel_id=1, source_target_pairs={{0,4},{4,8},{8,12},{12,16},{16,20},{20,24},{24,28},{28,32},{32,36}... | collective-permute-start | bytes 46088 | tf_op jit(solution)/shard_map/ppermute | solution.py:15
  192.5 7.2 %collective-permute-start.1 = (bf16[15,512]{1,0:T(8,128)(2,1)S(1)}, bf16[15,512]{1,0:T(8,128)(2,1)S(1)}, u32[]{:S(2)}, u32[]{:S(2)}) collective-permute-start(bf16[15,512]{1,0:T(8,128)(2,1)S(1)} %get-tuple-element.151), channel_id=1, source_target_pairs={{4,0},{8,4},{12,8},{16,12},{20,16},{24,20},{28,24},{32,28},{36,32}... | collective-permute-start | bytes 46088 | tf_op jit(solution)/shard_map/ppermute | solution.py:18
